TPU v7x, 32 devices: a whole 2x2x4 slice. The times are simulated.
32 devices in a mesh: row: 4 (over y, x), col: 8 (over z, core).
Axes of the slice: x: 2, y: 2, z: 4, core: 2. Of those that a mesh axis runs over, the one named last changes fastest.
Arguments:
- trailing_grad: bfloat16 [4, 8, 768, 24576], P(None, 'col', None, 'row'), may hold values from -6 to 6
- panel: bfloat16 [24576, 512], P(('row', 'col')), may hold values from -0.0390625 to 0.0390625
- panel_grad: float32 [24576, 512], P(('row', 'col')), may hold values from -6 to 6
- diag_factor: float32 [512, 512], replicated, may hold values from -2 to 2, as said below
- diag_grad: float32 [512, 512], replicated, may hold values from -6 to 6
Outputs:
- panel_adj: float32 [24576, 512], P(('row', 'col'))
- diag_adj: float32 [512, 512], replicated
Inputs may be any that keep to these rules, and one draw needn't show every extreme that they name: `diag_factor`: lower triangular with zeros above the diagonal; diagonal entries between 1 and 2.
All inputs are finite; a program needn't handle non-finite values.
Results may differ from a plain program's by a relative error of at most 0.0003.
Values may be sent and summed in bfloat16 or wider, within the bound.
A program may use at most 128 MiB of HBM per device.

v0:
```python
import jax
import jax.numpy as jnp
from jax import lax
from jax.sharding import PartitionSpec as P


def halve_lower(matrix):
    rows = lax.broadcasted_iota(jnp.int32, matrix.shape, 0)
    cols = lax.broadcasted_iota(jnp.int32, matrix.shape, 1)
    keep = jnp.where(rows > cols, 1.0, jnp.where(rows == cols, 0.5, 0.0)).astype(jnp.float32)
    return matrix * keep


def keep_lower(matrix):
    rows = lax.broadcasted_iota(jnp.int32, matrix.shape, 0)
    cols = lax.broadcasted_iota(jnp.int32, matrix.shape, 1)
    return jnp.where(rows >= cols, matrix, 0.0)


def right_solve(left, lower):
    right = jax.scipy.linalg.solve_triangular(lower, left.T, lower=True, trans=1).T
    return 0.5 * (right + right.T)


def on_device(trailing_grad, panel, panel_grad, diag_factor, diag_grad):
    local_flip = trailing_grad.reshape(-1, trailing_grad.shape[3])
    lower = jnp.tril(diag_factor)
    col_panel = lax.all_gather(panel, "row", axis=0, tiled=True)
    row_panel = lax.all_gather(panel, "col", axis=0, tiled=True)
    block = local_flip
    direct = lax.psum_scatter(
        lax.dot_general(
            block, col_panel, (((0,), (0,)), ((), ())), preferred_element_type=jnp.float32
        ),
        "col",
        scatter_dimension=0,
        tiled=True,
    )
    block = local_flip
    transposed = lax.psum_scatter(
        jnp.dot(block, row_panel, preferred_element_type=jnp.float32),
        "row",
        scatter_dimension=0,
        tiled=True,
    )
    reduced = panel_grad - direct - transposed
    panel_adj = jax.scipy.linalg.solve_triangular(lower, reduced.T, lower=True, trans=1).T
    contrib = lax.dot_general(
        panel_adj,
        panel.astype(jnp.float32),
        (((0,), (0,)), ((), ())),
        precision=lax.Precision.HIGHEST,
    )
    diag_new = diag_grad - lax.psum(contrib, ("row", "col"))
    inner = halve_lower(jnp.dot(lower.T, keep_lower(diag_new), precision=lax.Precision.HIGHEST))
    left = jax.scipy.linalg.solve_triangular(lower, inner, lower=True, trans=1)
    return (panel_adj, right_solve(left, lower))


def solution(mesh):
    in_specs = (
        P(None, "col", None, "row"),
        P(("row", "col"), None),
        P(("row", "col"), None),
        P(),
        P(),
    )
    out_specs = (P(("row", "col"), None), P())
    return jax.shard_map(
        on_device, mesh=mesh, in_specs=in_specs, out_specs=out_specs, check_vma=False
    )
```

profile of v0, /device:TPU:0, one launch (start us, length us, event | category | flops | bytes accessed | tf_op | source)
XLA Modules:
  0.0 489.1 jit_solution(2284740775558172705)
XLA Ops:
  8.7 68.4 %all-gather.5.cloned.1.call-done = bf16[6144,512]{1,0:T(8,128)(2,1)} async-done(((bf16[768,512]{1,0:T(8,128)(2,1)}), bf16[6144,512]{1,0:T(8,128)(2,1)}) %all-gather.5.cloned.1.call-update) | async-done | bytes 6291472 | tf_op jit(solution)/shard_map/all_gather | solution.py:29
  77.1 26.8 %fusion.67 = f32[3072,512]{1,0:T(8,128)} fusion(bf16[3072,6144]{1,0:T(8,128)(2,1)} %bitcast.70, bf16[6144,512]{1,0:T(8,128)(2,1)} %all-gather.5.cloned.1.call-done), kind=kOutput, calls=%fused_computation.91 | convolution fusion | flops 19327352832 | bytes 50331648 | tf_op jit(solution)/shard_map/dot_general | solution.py:41
  103.9 17.5 %all-gather.3.cloned.1.call-done = bf16[3072,512]{1,0:T(8,128)(2,1)} async-done(((bf16[768,512]{1,0:T(8,128)(2,1)}), bf16[3072,512]{1,0:T(8,128)(2,1)}) %all-gather.3.cloned.1.call-update) | async-done | bytes 3145744 | tf_op jit(solution)/shard_map/all_gather | solution.py:28
  121.4 27.7 %fusion.66 = f32[6144,512]{1,0:T(8,128)} fusion(bf16[3072,6144]{1,0:T(8,128)(2,1)} %bitcast.71, bf16[3072,512]{1,0:T(8,128)(2,1)} %all-gather.3.cloned.1.call-done), kind=kOutput, calls=%fused_computation.90 | convolution fusion | flops 19327352832 | bytes 53477376 | tf_op jit(solution)/shard_map/dot_general | solution.py:32
  149.2 1.1 copy-done.6
  150.5 8.0 %while.5 = (s32[]{:T(128)}, f32[512,512]{1,0:T(8,128)S(1)}, s32[4,2]{0,1:T(2,128)S(1)}, f32[4,128,128]{2,1,0:T(8,128)S(1)}, s32[]{:T(128)}) while((s32[]{:T(128)}, f32[512,512]{1,0:T(8,128)S(1)}, s32[4,2]{0,1:T(2,128)S(1)}, f32[4,128,128]{2,1,0:T(8,128)S(1)}, s32[]{:T(128)}) %tuple.32), condition=%wide.while_cond.1, body=%wide.while_body.1.sunk | while | flops 2 | bytes 131181 | solution.py:47
  151.1 1.4 bitcast_dynamic-update-slice_fusion.2
  153.1 1.3 bitcast_dynamic-update-slice_fusion.2
  155.1 1.3 bitcast_dynamic-update-slice_fusion.2
  157.1 1.3 bitcast_dynamic-update-slice_fusion.2
  158.5 39.5 %custom-call.7 = f32[4,128,128]{1,2,0:T(8,128)S(1)} custom-call(f32[4,128,128]{2,1,0:T(8,128)S(1)} %get-tuple-element.18), custom_call_target="InvertDiagBlocksLowerTriangular" | custom-call | tf_op jit(solution)/shard_map/jit(_solve_triangular)/triangular_solve | solution.py:47
  198.0 127.9 %reduce-scatter.3.cloned.1.call-done = f32[768,512]{1,0:T(8,128)} async-done(((f32[6144,512]{1,0:T(8,128)}), f32[768,512]{1,0:T(8,128)}) %reduce-scatter.3.cloned.1.call-update) | async-done | bytes 1572880 | tf_op jit(solution)/shard_map/reduce_scatter | solution.py:31
  325.9 2.9 subtract_bitcast_fusion
  330.6 1.4 convolution_subtract_fusion.2
  332.5 2.1 convolution_subtract_fusion
  334.7 1.2 fusion.47
  335.9 3.4 fusion.10
  339.3 1.2 fusion.11
  340.5 1.6 copy.8
  342.2 126.4 %all-reduce.2.cloned.1.call-done = f32[512,512]{1,0:T(8,128)} async-done(((f32[512,512]{1,0:T(8,128)}), f32[512,512]{1,0:T(8,128)}) %all-reduce.2.cloned.1.call-update) | async-done | bytes 1048592 | tf_op jit(solution)/shard_map/psum | solution.py:54
  468.6 3.7 convolution_multiply_fusion
  477.1 1.0 convolution_subtract_fusion.3
  478.5 1.5 convolution_subtract_fusion.7
  481.4 1.2 add_multiply_fusion
  (55 shorter events, 12.9 us)
Async XLA Ops:
  7.2 69.9 %all-gather.5.cloned.1.call-start = ((), (), s32[]{:S(2)}) async-start(), calls=%async_computation.4 | async-start | bytes 7077888 | tf_op jit(solution)/shard_map/all_gather | solution.py:29
  7.9 113.5 %all-gather.3.cloned.1.call-start = ((), (), s32[]{:S(2)}) async-start(), calls=%async_computation.2 | async-start | bytes 3932160 | tf_op jit(solution)/shard_map/all_gather | solution.py:28
  8.6 189.3 %reduce-scatter.5.cloned.1.call-start = ((), (), s32[]{:S(2)}) async-start(), calls=%async_computation.5 | async-start | bytes 7864320 | tf_op jit(solution)/shard_map/reduce_scatter | solution.py:40
  103.8 222.1 %reduce-scatter.3.cloned.1.call-start = ((), (), s32[]{:S(2)}) async-start(), calls=%async_computation.3 | async-start | bytes 14155776 | tf_op jit(solution)/shard_map/reduce_scatter | solution.py:31
  149.1 1.2 copy-start.6
  149.1 319.4 %all-reduce.2.cloned.1.call-start = ((), (), s32[]{:S(2)}) async-start(), calls=%async_computation.6 | async-start | bytes 2097152 | tf_op jit(solution)/shard_map/psum | solution.py:54
  198.0 136.7 %copy-start.4 = (f32[4,128,128]{1,2,0:T(8,128)}, f32[4,128,128]{1,2,0:T(8,128)S(1)}, u32[]{:S(2)}) copy-start(f32[4,128,128]{1,2,0:T(8,128)S(1)} %custom-call.7) | copy-start | bytes 786436
  332.5 3.4 copy-start.2
  332.5 3.4 copy-start.3
  342.2 130.1 %copy-start.5 = (f32[4,128,128]{1,2,0:T(8,128)S(1)}, f32[4,128,128]{1,2,0:T(8,128)}, u32[]{:S(2)}) copy-start(f32[4,128,128]{1,2,0:T(8,128)} %copy-done.4) | copy-start | bytes 786436
  478.4 1.9 copy-start
  480.4 1.0 copy-start.1
Sparse Core Ops, SparseCore 0:
  9.6 67.4 all-gather.4
  78.9 42.4 all-gather.2
  124.4 70.1 reduce-scatter.4
  196.8 129.1 reduce-scatter.2
  339.4 129.0 all-reduce.1
where the time goes:
time: 489 us
  waiting for transfers between devices  342 us (70%)
  matrix products  76.4 us (16%)
  other arithmetic  45.1 us (9%)
  between operations  14.1 us (3%)
  local copies, waits for them, and re-layouts  11.6 us (2%)
    reduce_scatter x1, waiting for transfers between devices, on_device(): lax.psum_scatter(lax.dot_general(block, col_panel, (((0,), (0,)), ((), ()...  128 us
    psum x1, waiting for transfers between devices, on_device(): diag_new = diag_grad - lax.psum(contrib, ('row', 'col'))  126 us
    all_gather x1, waiting for transfers between devices, on_device(): row_panel = lax.all_gather(panel, 'col', axis=0, tiled=True)  68.4 us
    another operation x3, other arithmetic, on_device(): jax.scipy.linalg.solve_triangular(lower, reduced.T, lower=True, trans=1)  39.6 us
    dot_general x1, matrix products, on_device(): lax.dot_general(block, col_panel, (((0,), (0,)), ((), ())), preferred_ele...  27.7 us
    dot_general x1, matrix products, on_device(): jnp.dot(block, row_panel, preferred_element_type=jnp.float32)  26.8 us
    all_gather x1, waiting for transfers between devices, on_device(): col_panel = lax.all_gather(panel, 'row', axis=0, tiled=True)  17.5 us
  transfers between devices with their start and end apart: 5, of which 4 were waited for; matrix products, arithmetic and copies ran while one was open for 21% of the time, Pallas kernels for 0%

commit v1 on v0

--- a/solution.py
+++ b/solution.py
@@ -26,7 +26,9 @@
     local_flip = trailing_grad.reshape(-1, trailing_grad.shape[3])
     lower = jnp.tril(diag_factor)
     col_panel = lax.all_gather(panel, "row", axis=0, tiled=True)
-    row_panel = lax.all_gather(panel, "col", axis=0, tiled=True)
+    row_panel = jnp.concatenate(
+        lax.all_to_all(jnp.stack([panel] * lax.axis_size("col")), "col", 0, 0), axis=0
+    )
     block = local_flip
     direct = lax.psum_scatter(
         lax.dot_general(

time: 489 us -> 547 us (1.12)
  waiting for transfers between devices: 342 us -> 390 us
  starting transfers between devices: 0.2 us -> 6.51 us
    all_to_all x0 -> x1, waiting for transfers between devices: none -> 138 us  [on_device(): lax.all_to_all(jnp.stack([panel] * lax.axis_size('col')), 'col', 0, 0)]
    all_gather x1 -> x0, waiting for transfers between devices: 68.4 us -> none  [on_device(): row_panel = lax.all_gather(panel, 'col', axis=0, tiled=True)]
    all_gather x1, waiting for transfers between devices: 17.5 us -> 0.02 us  [on_device(): col_panel = lax.all_gather(panel, 'row', axis=0, tiled=True)]
    all_to_all x0 -> x1, starting transfers between devices: none -> 6.35 us  [on_device(): lax.all_to_all(jnp.stack([panel] * lax.axis_size('col')), 'col', 0, 0)]
    another operation x12 -> x13, local copies, waits for them, and re-layouts: 7.88 us -> 12.2 us
  transfers between devices with their start and end apart: 5 -> 5, of which waited for: 4 -> 3; matrix products, arithmetic and copies ran while one was open for 21% -> 19% of each run, Pallas kernels for 0% -> 0%
where the time goes in v1:
time: 547 us
  waiting for transfers between devices  390 us (71%)
  matrix products  74.6 us (14%)
  other arithmetic  45.1 us (8%)
  local copies, waits for them, and re-layouts  16.7 us (3%)
  between operations  14.1 us (3%)
  starting transfers between devices  6.51 us (1%)
    all_to_all x1, waiting for transfers between devices, on_device(): lax.all_to_all(jnp.stack([panel] * lax.axis_size('col')), 'col', 0, 0)  138 us
    psum x1, waiting for transfers between devices, on_device(): diag_new = diag_grad - lax.psum(contrib, ('row', 'col'))  126 us
    reduce_scatter x1, waiting for transfers between devices, on_device(): lax.psum_scatter(lax.dot_general(block, col_panel, (((0,), (0,)), ((), ()...  124 us
    another operation x3, other arithmetic, on_device(): jax.scipy.linalg.solve_triangular(lower, reduced.T, lower=True, trans=1)  39.6 us
    dot_general x1, matrix products, on_device(): lax.dot_general(block, col_panel, (((0,), (0,)), ((), ())), preferred_ele...  27.7 us
    dot_general x1, matrix products, on_device(): jnp.dot(block, row_panel, preferred_element_type=jnp.float32)  26.7 us
  transfers between devices with their start and end apart: 5, of which 3 were waited for; matrix products, arithmetic and copies ran while one was open for 19% of the time, Pallas kernels for 0%

profile of v1, /device:TPU:0, one launch (start us, length us, event | category | flops | bytes accessed | tf_op | source)
XLA Modules:
  0.0 546.5 jit_solution(8519087662315249348)
XLA Ops:
  7.2 4.3 stack.2
  11.5 6.4 %all-to-all-start = ((bf16[8,768,512]{2,1,0:T(8,128)(2,1)}), bf16[8,768,512]{2,1,0:T(8,128)(2,1)}, u32[]{:S(2)}, u32[]{:S(2)}) async-start(bf16[8,768,512]{2,1,0:T(8,128)(2,1)} %stack.2), calls=%async_computation.1 | async-start | bytes 12582912 | tf_op jit(solution)/shard_map/all_to_all | solution.py:30
  18.6 138.2 %all-to-all-done = bf16[8,768,512]{2,1,0:T(8,128)(2,1)} async-done(((bf16[8,768,512]{2,1,0:T(8,128)(2,1)}), bf16[8,768,512]{2,1,0:T(8,128)(2,1)}, u32[]{:S(2)}, u32[]{:S(2)}) %all-to-all-start) | async-done | bytes 6291488 | tf_op jit(solution)/shard_map/all_to_all | solution.py:30
  156.9 26.7 %fusion.67 = f32[3072,512]{1,0:T(8,128)} fusion(bf16[3072,6144]{1,0:T(8,128)(2,1)} %bitcast.71, bf16[6144,512]{1,0:T(8,128)(2,1)} %bitcast.2), kind=kOutput, calls=%fused_computation.91 | convolution fusion | flops 19327352832 | bytes 50331648 | tf_op jit(solution)/shard_map/dot_general | solution.py:43
  183.7 27.7 %fusion.66 = f32[6144,512]{1,0:T(8,128)} fusion(bf16[3072,6144]{1,0:T(8,128)(2,1)} %bitcast.72, bf16[3072,512]{1,0:T(8,128)(2,1)} %all-gather.2.cloned.1.call-done), kind=kOutput, calls=%fused_computation.90 | convolution fusion | flops 19327352832 | bytes 53477376 | tf_op jit(solution)/shard_map/dot_general | solution.py:34
  211.5 1.1 copy-done.7
  212.8 8.0 %while.5 = (s32[]{:T(128)}, f32[512,512]{1,0:T(8,128)S(1)}, s32[4,2]{0,1:T(2,128)S(1)}, f32[4,128,128]{2,1,0:T(8,128)S(1)}, s32[]{:T(128)}) while((s32[]{:T(128)}, f32[512,512]{1,0:T(8,128)S(1)}, s32[4,2]{0,1:T(2,128)S(1)}, f32[4,128,128]{2,1,0:T(8,128)S(1)}, s32[]{:T(128)}) %tuple.32), condition=%wide.while_cond.1, body=%wide.while_body.1.sunk | while | flops 2 | bytes 131189 | solution.py:49
  213.4 1.3 bitcast_dynamic-update-slice_fusion.2
  215.4 1.3 bitcast_dynamic-update-slice_fusion.2
  217.4 1.3 bitcast_dynamic-update-slice_fusion.2
  219.4 1.3 bitcast_dynamic-update-slice_fusion.2
  220.7 39.5 %custom-call.7 = f32[4,128,128]{1,2,0:T(8,128)S(1)} custom-call(f32[4,128,128]{2,1,0:T(8,128)S(1)} %get-tuple-element.18), custom_call_target="InvertDiagBlocksLowerTriangular" | custom-call | tf_op jit(solution)/shard_map/jit(_solve_triangular)/triangular_solve | solution.py:49
  260.3 124.1 %reduce-scatter.3.cloned.1.call-done = f32[768,512]{1,0:T(8,128)} async-done(((f32[6144,512]{1,0:T(8,128)}), f32[768,512]{1,0:T(8,128)}) %reduce-scatter.3.cloned.1.call-update) | async-done | bytes 1572880 | tf_op jit(solution)/shard_map/reduce_scatter | solution.py:33
  384.4 2.9 subtract_bitcast_fusion
  389.1 1.4 convolution_subtract_fusion.2
  391.0 2.1 convolution_subtract_fusion
  394.4 2.4 fusion.10
  396.8 1.2 fusion.11
  398.0 1.6 copy.8
  399.6 126.4 %all-reduce.2.cloned.1.call-done = f32[512,512]{1,0:T(8,128)} async-done(((f32[512,512]{1,0:T(8,128)}), f32[512,512]{1,0:T(8,128)}) %all-reduce.2.cloned.1.call-update) | async-done | bytes 1048592 | tf_op jit(solution)/shard_map/psum | solution.py:56
  526.0 3.7 convolution_multiply_fusion
  534.5 1.0 convolution_subtract_fusion.3
  535.9 1.5 convolution_subtract_fusion.7
  538.8 1.2 add_multiply_fusion
  (57 shorter events, 13.4 us)
Async XLA Ops:
  11.5 145.4 %all-to-all-start = ((bf16[8,768,512]{2,1,0:T(8,128)(2,1)}), bf16[8,768,512]{2,1,0:T(8,128)(2,1)}, u32[]{:S(2)}, u32[]{:S(2)}) async-start(bf16[8,768,512]{2,1,0:T(8,128)(2,1)} %stack.2), calls=%async_computation.1 | async-start | bytes 12582912 | tf_op jit(solution)/shard_map/all_to_all | solution.py:30
  17.8 165.9 %all-gather.2.cloned.1.call-start = ((), (), s32[]{:S(2)}) async-start(), calls=%async_computation.3 | async-start | bytes 3932160 | tf_op jit(solution)/shard_map/all_gather | solution.py:28
  18.6 241.7 %reduce-scatter.5.cloned.1.call-start = ((), (), s32[]{:S(2)}) async-start(), calls=%async_computation.5 | async-start | bytes 7864320 | tf_op jit(solution)/shard_map/reduce_scatter | solution.py:42
  183.6 200.7 %reduce-scatter.3.cloned.1.call-start = ((), (), s32[]{:S(2)}) async-start(), calls=%async_computation.4 | async-start | bytes 14155776 | tf_op jit(solution)/shard_map/reduce_scatter | solution.py:33
  211.4 1.2 copy-start.7
  211.4 314.6 %all-reduce.2.cloned.1.call-start = ((), (), s32[]{:S(2)}) async-start(), calls=%async_computation.6 | async-start | bytes 2097152 | tf_op jit(solution)/shard_map/psum | solution.py:56
  260.3 132.8 %copy-start.4 = (f32[4,128,128]{1,2,0:T(8,128)}, f32[4,128,128]{1,2,0:T(8,128)S(1)}, u32[]{:S(2)}) copy-start(f32[4,128,128]{1,2,0:T(8,128)S(1)} %custom-call.7) | copy-start | bytes 786436
  391.0 2.6 copy-start.2
  391.0 3.4 copy-start.3
  393.6 0.8 copy-start.6
  399.6 130.1 %copy-start.5 = (f32[4,128,128]{1,2,0:T(8,128)S(1)}, f32[4,128,128]{1,2,0:T(8,128)}, u32[]{:S(2)}) copy-start(f32[4,128,128]{1,2,0:T(8,128)} %copy-done.4) | copy-start | bytes 786436
  535.9 1.9 copy-start
  537.8 1.0 copy-start.1
Sparse Core Ops, SparseCore 0:
  20.5 45.2 all-gather.1
  183.7 69.1 reduce-scatter.4
  255.2 129.0 reduce-scatter.2
  396.9 129.0 all-reduce.1
